TPU v7x, 256 devices: a whole 4x4x8 slice. The times are simulated.
256 devices in a mesh: dom: 32 (over x, y, core), tm: 8 (over z).
Axes of the slice: x: 4, y: 4, z: 8, core: 2. Of those that a mesh axis runs over, the one named last changes fastest.
Arguments:
- features: bfloat16 [8, 8192, 512], P('tm', 'dom'), may hold values from -6 to 6
- tile_rows: int32 [8, 768], P('tm', 'dom'), may hold values from 0 to 63, as said below
- tile_cols: int32 [8, 768], P('tm', 'dom'), may hold values from 0 to 63, as said below
- tile_vals: bfloat16 [8, 768, 128, 128], P('tm', 'dom'), may hold values from 0 to 0.0625
- tile_used: int32 [8, 32], P('tm', 'dom'), may hold values from 12 to 24, as said below
- pool_weight: bfloat16 [512, 512], replicated, may hold values from -0.25 to 0.25
- w_in: bfloat16 [3, 512, 512], replicated, may hold values from -0.25 to 0.25
- w_state: bfloat16 [3, 512, 512], replicated, may hold values from -0.25 to 0.25
- gate_offset: float32 [512], replicated, may hold values from 0 to 5
- start_weight: float32 [512, 512], replicated, may hold values from -3 to 3
Outputs:
- hidden_out: bfloat16 [8, 8192, 512], P('tm', 'dom')
- weights_out: float32 [8, 512, 512], P('tm')
Inputs may be any that keep to these rules, and one draw needn't show every extreme that they name: `tile_rows`: every slot of row partition d names a row block of that partition, d * 2 to (d + 1) * 2 - 1. `tile_cols`: within one snapshot and one row partition, all slots whose column blocks lie on the same dom index name the same column block. `tile_used`: in every snapshot some row partition has all 24 slots live.
All inputs are finite; a program needn't handle non-finite values.
Results may differ from a plain program's by a relative error of at most 0.017.
Values may be sent and summed in bfloat16 or wider, within the bound.
No kernel may reach another device: no remote copies, remote signals or barrier semaphores. Data moves between devices by JAX's collectives and lax.ppermute only.
A program may use at most 64 MiB of HBM per device.

v0:
```python
import jax
import jax.numpy as jnp
from jax import lax
from jax.sharding import PartitionSpec as P

BLOCK = 128


def shifted(block, axis, distance):
    devices = range(lax.axis_size(axis))
    route = [(i - distance, i) for i in devices if i - distance in devices]
    return lax.ppermute(block, axis, route)


def gru_step(state, inputs_t, w_state, gate_offset):
    state_b = state.astype(jnp.bfloat16)
    upd_pre = jnp.dot(w_state[0], state_b, preferred_element_type=jnp.float32)
    rst_pre = jnp.dot(w_state[1], state_b, preferred_element_type=jnp.float32)
    update = jax.nn.sigmoid(inputs_t[0] + upd_pre - gate_offset[:, None])
    reset = jax.nn.sigmoid(inputs_t[1] + rst_pre)
    reset_state = (reset * state).astype(jnp.bfloat16)
    candidate = jnp.tanh(
        inputs_t[2] + jnp.dot(w_state[2], reset_state, preferred_element_type=jnp.float32)
    )
    return (1.0 - update) * state + update * candidate


def shards(
    features,
    tile_rows,
    tile_cols,
    tile_vals,
    tile_used,
    pool_weight,
    w_in,
    w_state,
    gate_offset,
    start_weight,
):
    snap_dev, rows_dev, width = features.shape
    slots = tile_rows.shape[1]
    n_dom = lax.axis_size("dom")
    n_tm = lax.axis_size("tm")
    dom_index = lax.axis_index("dom")
    tm_index = lax.axis_index("tm")
    blocks_dev = rows_dev // BLOCK
    local_rows = tile_rows - dom_index * blocks_dev
    owner_dev = tile_cols // blocks_dev
    block_pick = tile_cols % blocks_dev
    live_mask = jnp.arange(slots, dtype=jnp.int32)[None, :] < tile_used
    peer_ids = jnp.arange(n_dom, dtype=jnp.int32)
    matches = (owner_dev[:, None, :] == peer_ids[None, :, None]) & live_mask[:, None, :]
    wanted_block = jnp.max(jnp.where(matches, block_pick[:, None, :], 0), axis=2)
    snap_base = (jnp.arange(snap_dev, dtype=jnp.int32) * blocks_dev)[:, None]
    wanted = (wanted_block + snap_base).T
    flat_blocks = features.reshape(snap_dev * blocks_dev, BLOCK, width)
    replies = jnp.take(
        flat_blocks, lax.all_to_all(wanted, "dom", split_axis=0, concat_axis=0, tiled=True), axis=0
    )
    fetched = lax.all_to_all(replies, "dom", split_axis=0, concat_axis=0, tiled=True)

    def source_of(s, j):
        return fetched[owner_dev[s, j], s]

    s = 0
    totals = features[s].astype(jnp.float32).reshape(blocks_dev, BLOCK, width)

    def add_tile(j, totals, s=s):
        product = jnp.dot(tile_vals[s, j], source_of(s, j), preferred_element_type=jnp.float32)
        return totals.at[local_rows[s, j]].add(product)

    totals = lax.fori_loop(0, tile_used[s, 0], add_tile, totals)
    aggregated = [totals.reshape(rows_dev, width).astype(jnp.bfloat16)]
    s = 0
    pool_gates = jax.nn.sigmoid(
        jnp.dot(features[s], pool_weight, preferred_element_type=jnp.float32)
    ).astype(jnp.bfloat16)
    partial_pool = [
        jnp.einsum("nd,nk->dk", features[s], pool_gates, preferred_element_type=jnp.float32)
    ]
    pooled = lax.psum(jnp.stack(partial_pool).astype(jnp.bfloat16), "dom").astype(jnp.float32)
    summary = (pooled * (rows_dev * n_dom) ** (-0.5)).astype(jnp.bfloat16)
    in_side = jnp.einsum("gij,tjk->tgik", w_in, summary, preferred_element_type=jnp.float32)

    def run_final(state):
        state = gru_step(state, in_side[0], w_state, gate_offset)
        return state

    def keep_state(state):
        return state

    state = start_weight
    for k in range(n_tm - 1):
        final = lax.cond(tm_index == k, run_final, keep_state, state)
        incoming = shifted(final.astype(jnp.bfloat16), "tm", 1).astype(final.dtype)
        state = jnp.where(tm_index == k + 1, incoming, state)
    s = 0
    state = gru_step(state, in_side[s], w_state, gate_offset)
    history = [state]
    evolved = jnp.stack(history)
    s = 0
    mixed = jnp.dot(
        aggregated[s], evolved[s].astype(jnp.bfloat16), preferred_element_type=jnp.float32
    )
    outputs = [jnp.maximum(mixed * width ** (-0.5), 0.0).astype(jnp.bfloat16)]
    return (jnp.stack(outputs), evolved)


def solution(mesh):
    in_specs = (
        P("tm", "dom", None),
        P("tm", "dom"),
        P("tm", "dom"),
        P("tm", "dom", None, None),
        P("tm", "dom"),
        P(),
        P(),
        P(),
        P(),
        P(),
    )
    out_specs = (P("tm", "dom", None), P("tm", None, None))
    return jax.shard_map(shards, mesh=mesh, in_specs=in_specs, out_specs=out_specs, check_vma=False)
```

profile of v0, /device:TPU:162, one launch (start us, length us, event | category | flops | bytes accessed | tf_op | source)
XLA Modules:
  0.0 496.8 jit_solution(9960098003639466256)
XLA Ops:
  7.2 2.8 fusion.220
  10.1 116.7 %all-reduce.2.cloned.1.call-done = bf16[1,512,512]{1,2,0:T(8,128)(2,1)} async-done(((bf16[1,512,512]{1,2,0:T(8,128)(2,1)}), bf16[1,512,512]{1,2,0:T(8,128)(2,1)}) %all-reduce.2.cloned.1.call-update) | async-done | bytes 524304 | tf_op jit(solution)/shard_map/psum | solution.py:81
  126.8 3.7 convolution_bitcast_fusion.8
  130.8 2.6 collective-permute-start
  135.3 11.3 %collective-permute-done = bf16[512,512]{0,1:T(8,128)(2,1)S(1)} collective-permute-done((bf16[512,512]{0,1:T(8,128)(2,1)S(1)}, bf16[512,512]{0,1:T(8,128)(2,1)S(1)}, u32[]{:S(2)}, u32[]{:S(2)}) %collective-permute-start) | collective-permute-done | bytes 524320 | tf_op jit(solution)/shard_map/ppermute | solution.py:12
  148.5 2.6 collective-permute-start.1
  151.9 6.2 %all-to-all-start = ((s32[32,1,1]{2,1,0:T(1,128)}), s32[32,1,1]{2,1,0:T(1,128)S(1)}, u32[]{:S(2)}, u32[]{:S(2)}) async-start(s32[32,1,1]{2,1,0:T(1,128)} %copy.126), calls=%async_computation | async-start | bytes 32768 | tf_op jit(solution)/shard_map/all_to_all | solution.py:58
  158.2 6.1 %all-to-all-done = s32[32,1,1]{2,1,0:T(1,128)S(1)} async-done(((s32[32,1,1]{2,1,0:T(1,128)}), s32[32,1,1]{2,1,0:T(1,128)S(1)}, u32[]{:S(2)}, u32[]{:S(2)}) %all-to-all-start) | async-done | bytes 160 | tf_op jit(solution)/shard_map/all_to_all | solution.py:58
  166.2 2.6 collective-permute-start.2
  168.8 2.8 gather_fusion
  171.7 4.7 bitcast_select_fusion
  176.3 6.1 %all-to-all-start.1 = ((bf16[32,1,128,512]{3,2,1,0:T(8,128)(2,1)}), bf16[32,1,128,512]{3,2,1,0:T(8,128)(2,1)}, u32[]{:S(2)}, u32[]{:S(2)}) async-start(bf16[32,1,128,512]{3,2,1,0:T(8,128)(2,1)} %bitcast_select_fusion), calls=%async_computation.1 | async-start | bytes 8388608 | tf_op jit(solution)/shard_map/all_to_all | solution.py:60
  185.0 14.1 %collective-permute-done.3 = bf16[512,512]{0,1:T(8,128)(2,1)S(1)} collective-permute-done((bf16[512,512]{0,1:T(8,128)(2,1)S(1)}, bf16[512,512]{0,1:T(8,128)(2,1)S(1)}, u32[]{:S(2)}, u32[]{:S(2)}) %collective-permute-start.3) | collective-permute-done | bytes 524320 | tf_op jit(solution)/shard_map/ppermute | solution.py:12
  201.7 51.7 %collective-permute-done.4 = bf16[512,512]{0,1:T(8,128)(2,1)S(1)} collective-permute-done((bf16[512,512]{0,1:T(8,128)(2,1)S(1)}, bf16[512,512]{0,1:T(8,128)(2,1)S(1)}, u32[]{:S(2)}, u32[]{:S(2)}) %collective-permute-start.4) | collective-permute-done | bytes 524320 | tf_op jit(solution)/shard_map/ppermute | solution.py:12
  253.6 10.0 %conditional.12 = (bf16[512,512]{1,0:T(8,128)(2,1)S(1)}) conditional(s32[]{:T(128)} %convert_element_type.155, (f32[512,512]{0,1:T(8,128)S(1)}) %tuple.103, (f32[1,3,512,512]{2,3,1,0:T(8,128)}, bf16[3,512,512]{2,1,0:T(8,128)(2,1)}, f32[512,512]{0,1:T(8,128)S(1)}, f32[512]{0:T(512)S(1)}) %tuple.144), branch_computations={%region_15.16_spmd, %region_16.17_spmd} | conditional | flops 810287104 | bytes 19925000 | solution.py:94
  253.6 3.6 copy.147
  257.5 3.0 fusion.161
  260.5 3.1 fusion.151
  265.8 11.3 %collective-permute-done.5 = bf16[512,512]{0,1:T(8,128)(2,1)S(1)} collective-permute-done((bf16[512,512]{0,1:T(8,128)(2,1)S(1)}, bf16[512,512]{0,1:T(8,128)(2,1)S(1)}, u32[]{:S(2)}, u32[]{:S(2)}) %collective-permute-start.5) | collective-permute-done | bytes 524320 | tf_op jit(solution)/shard_map/ppermute | solution.py:12
  277.6 12.2 %collective-permute-start.6 = (bf16[512,512]{0,1:T(8,128)(2,1)S(1)}, bf16[512,512]{0,1:T(8,128)(2,1)S(1)}, u32[]{:S(2)}, u32[]{:S(2)}) collective-permute-start(bf16[512,512]{0,1:T(8,128)(2,1)S(1)} %copy.153), channel_id=1, source_target_pairs={{0,1},{1,2},{2,3},{3,4},{4,5},{5,6},{6,7},{8,9},{9,10},{10,11},{11... | collective-permute-start | bytes 1572872 | tf_op jit(solution)/shard_map/ppermute | solution.py:12
  289.9 7.9 %collective-permute-done.6 = bf16[512,512]{0,1:T(8,128)(2,1)S(1)} collective-permute-done((bf16[512,512]{0,1:T(8,128)(2,1)S(1)}, bf16[512,512]{0,1:T(8,128)(2,1)S(1)}, u32[]{:S(2)}, u32[]{:S(2)}) %collective-permute-start.6) | collective-permute-done | bytes 524320 | tf_op jit(solution)/shard_map/ppermute | solution.py:12
  297.8 3.0 fusion.218
  300.8 3.2 multiply_add_fusion
  305.3 182.2 %while.11 = (s32[]{:T(128)}, f32[2,128,512]{2,1,0:T(8,128)S(1)}, s32[]{:T(128)}, s32[1,24]{1,0:T(1,128)S(1)}, bf16[1,24,128,128]{3,2,1,0:T(8,128)(2,1)}, /*index...) while((s32[]{:T(128)}, f32[2,128,512]{2,1,0:T(8,128)S(1)}, ...), condition=%wide.region_3.4_spmd, body=%wide.region_1.3_spmd.sunk | while | flops 16908316 | bytes 689444 | solution.py:72
  (137 shorter events, 94.5 us)
Async XLA Ops:
  7.2 119.6 %copy-start = (bf16[3,512,512]{2,1,0:T(8,128)(2,1)S(1)}, bf16[3,512,512]{2,1,0:T(8,128)(2,1)}, u32[]{:S(2)}) copy-start(bf16[3,512,512]{2,1,0:T(8,128)(2,1)} %param.34) | copy-start | bytes 4718596
  7.2 119.6 %all-reduce.2.cloned.1.call-start = ((), (), s32[]{:S(2)}) async-start(), calls=%async_computation.2 | async-start | bytes 1048576 | tf_op jit(solution)/shard_map/psum | solution.py:81
  10.0 120.5 %copy-start.3 = (f32[512,512]{1,0:T(8,128)S(1)}, f32[512,512]{1,0:T(8,128)}, u32[]{:S(2)}) copy-start(f32[512,512]{1,0:T(8,128)} %param.37) | copy-start | bytes 3145732
  10.0 120.5 %copy-start.8 = (f32[512]{0:T(512)S(1)}, f32[512]{0:T(512)}, u32[]{:S(2)}) copy-start(f32[512]{0:T(512)} %param.36) | copy-start | bytes 6148
  130.8 15.8 %collective-permute-start = (bf16[512,512]{0,1:T(8,128)(2,1)S(1)}, bf16[512,512]{0,1:T(8,128)(2,1)S(1)}, u32[]{:S(2)}, u32[]{:S(2)}) collective-permute-start(bf16[512,512]{0,1:T(8,128)(2,1)S(1)} %copy.128), channel_id=1, source_target_pairs={{0,1},{1,2},{2,3},{3,4},{4,5},{5,6},{6,7},{8,9},{9,10},{10,11},{11... | collective-permute-start | bytes 1572872 | tf_op jit(solution)/shard_map/ppermute | solution.py:12
  148.0 3.0 copy-start.9
  148.5 17.1 %collective-permute-start.1 = (bf16[512,512]{0,1:T(8,128)(2,1)S(1)}, bf16[512,512]{0,1:T(8,128)(2,1)S(1)}, u32[]{:S(2)}, u32[]{:S(2)}) collective-permute-start(bf16[512,512]{0,1:T(8,128)(2,1)S(1)} %copy.133), channel_id=1, source_target_pairs={{0,1},{1,2},{2,3},{3,4},{4,5},{5,6},{6,7},{8,9},{9,10},{10,11},{11... | collective-permute-start | bytes 1572872 | tf_op jit(solution)/shard_map/ppermute | solution.py:12
  151.9 12.4 %all-to-all-start = ((s32[32,1,1]{2,1,0:T(1,128)}), s32[32,1,1]{2,1,0:T(1,128)S(1)}, u32[]{:S(2)}, u32[]{:S(2)}) async-start(s32[32,1,1]{2,1,0:T(1,128)} %copy.126), calls=%async_computation | async-start | bytes 32768 | tf_op jit(solution)/shard_map/all_to_all | solution.py:58
  166.0 2.8 copy-start.2
  166.2 16.2 %collective-permute-start.2 = (bf16[512,512]{0,1:T(8,128)(2,1)S(1)}, bf16[512,512]{0,1:T(8,128)(2,1)S(1)}, u32[]{:S(2)}, u32[]{:S(2)}) collective-permute-start(bf16[512,512]{0,1:T(8,128)(2,1)S(1)} %copy.137), channel_id=1, source_target_pairs={{0,1},{1,2},{2,3},{3,4},{4,5},{5,6},{6,7},{8,9},{9,10},{10,11},{11... | collective-permute-start | bytes 1572872 | tf_op jit(solution)/shard_map/ppermute | solution.py:12
  176.3 129.0 %all-to-all-start.1 = ((bf16[32,1,128,512]{3,2,1,0:T(8,128)(2,1)}), bf16[32,1,128,512]{3,2,1,0:T(8,128)(2,1)}, u32[]{:S(2)}, u32[]{:S(2)}) async-start(bf16[32,1,128,512]{3,2,1,0:T(8,128)(2,1)} %bitcast_select_fusion), calls=%async_computation.1 | async-start | bytes 8388608 | tf_op jit(solution)/shard_map/all_to_all | solution.py:60
  183.1 16.1 %collective-permute-start.3 = (bf16[512,512]{0,1:T(8,128)(2,1)S(1)}, bf16[512,512]{0,1:T(8,128)(2,1)S(1)}, u32[]{:S(2)}, u32[]{:S(2)}) collective-permute-start(bf16[512,512]{0,1:T(8,128)(2,1)S(1)} %copy.141), channel_id=1, source_target_pairs={{0,1},{1,2},{2,3},{3,4},{4,5},{5,6},{6,7},{8,9},{9,10},{10,11},{11... | collective-permute-start | bytes 1572872 | tf_op jit(solution)/shard_map/ppermute | solution.py:12
  199.7 53.7 %collective-permute-start.4 = (bf16[512,512]{0,1:T(8,128)(2,1)S(1)}, bf16[512,512]{0,1:T(8,128)(2,1)S(1)}, u32[]{:S(2)}, u32[]{:S(2)}) collective-permute-start(bf16[512,512]{0,1:T(8,128)(2,1)S(1)} %copy.145), channel_id=1, source_target_pairs={{0,1},{1,2},{2,3},{3,4},{4,5},{5,6},{6,7},{8,9},{9,10},{10,11},{11... | collective-permute-start | bytes 1572872 | tf_op jit(solution)/shard_map/ppermute | solution.py:12
  263.8 13.2 %collective-permute-start.5 = (bf16[512,512]{0,1:T(8,128)(2,1)S(1)}, bf16[512,512]{0,1:T(8,128)(2,1)S(1)}, u32[]{:S(2)}, u32[]{:S(2)}) collective-permute-start(bf16[512,512]{0,1:T(8,128)(2,1)S(1)} %copy.149), channel_id=1, source_target_pairs={{0,1},{1,2},{2,3},{3,4},{4,5},{5,6},{6,7},{8,9},{9,10},{10,11},{11... | collective-permute-start | bytes 1572872 | tf_op jit(solution)/shard_map/ppermute | solution.py:12
  277.4 12.5 %copy-start.10 = (s32[1,24]{1,0:T(1,128)S(1)}, s32[1,24]{1,0:T(1,128)}, u32[]{:S(2)}) copy-start(s32[1,24]{1,0:T(1,128)} %param.29) | copy-start | bytes 292
  277.6 20.2 %collective-permute-start.6 = (bf16[512,512]{0,1:T(8,128)(2,1)S(1)}, bf16[512,512]{0,1:T(8,128)(2,1)S(1)}, u32[]{:S(2)}, u32[]{:S(2)}) collective-permute-start(bf16[512,512]{0,1:T(8,128)(2,1)S(1)} %copy.153), channel_id=1, source_target_pairs={{0,1},{1,2},{2,3},{3,4},{4,5},{5,6},{6,7},{8,9},{9,10},{10,11},{11... | collective-permute-start | bytes 1572872 | tf_op jit(solution)/shard_map/ppermute | solution.py:12
  304.0 1.4 copy-start.4
  304.0 1.3 copy-start.7
  487.5 2.4 copy-start.1
Sparse Core Ops, SparseCore 0:
  11.8 114.9 all-reduce.1
where the time goes:
time: 500 us; the launch traced here: 497 us
  waiting for transfers between devices  219 us (44%)
  loops' own time  107 us (21%)
  matrix products  62.5 us (12%)
  starting transfers between devices  38.1 us (8%)
  local copies, waits for them, and re-layouts  28 us (6%)
  other arithmetic  26.7 us (5%)
  between operations  15.1 us (3%)
    psum x1, waiting for transfers between devices, shards(): lax.psum(jnp.stack(partial_pool).astype(jnp.bfloat16), 'dom')  117 us
    another operation x1, loops' own time, shards(): totals = lax.fori_loop(0, tile_used[s, 0], add_tile, totals)  107 us
    ppermute x7, waiting for transfers between devices, shifted(): return lax.ppermute(block, axis, route)  96.3 us
    dot_general x24, matrix products, add_tile(): jnp.dot(tile_vals[s, j], source_of(s, j), preferred_element_type=jnp.floa...  41.4 us
    ppermute x7, starting transfers between devices, shifted(): return lax.ppermute(block, axis, route)  25.7 us
    another operation x24, other arithmetic  18.3 us
    dynamic_slice x24, local copies, waits for them, and re-layouts, source_of(): return fetched[owner_dev[s, j], s]  15.4 us
  transfers between devices with their start and end apart: 10, of which 7 were waited for; matrix products, arithmetic and copies ran while one was open for 6% of the time, Pallas kernels for 0%

commit v1 on v0

--- a/solution.py
+++ b/solution.py
@@ -78,7 +78,9 @@
     partial_pool = [
         jnp.einsum("nd,nk->dk", features[s], pool_gates, preferred_element_type=jnp.float32)
     ]
-    pooled = lax.psum(jnp.stack(partial_pool).astype(jnp.bfloat16), "dom").astype(jnp.float32)
+    pooled = jnp.sum(
+        lax.all_gather(jnp.stack(partial_pool).astype(jnp.bfloat16), "dom"), axis=0
+    ).astype(jnp.float32)
     summary = (pooled * (rows_dev * n_dom) ** (-0.5)).astype(jnp.bfloat16)
     in_side = jnp.einsum("gij,tjk->tgik", w_in, summary, preferred_element_type=jnp.float32)
 

time: 500 us -> 483 us (0.966)
  waiting for transfers between devices: 219 us -> 183 us
  local copies, waits for them, and re-layouts: 28 us -> 40.6 us
  other arithmetic: 26.7 us -> 32.3 us
    psum x1 -> x0, waiting for transfers between devices: 117 us -> none  [shards(): lax.psum(jnp.stack(partial_pool).astype(jnp.bfloat16), 'dom')]
    all_gather x0 -> x1, waiting for transfers between devices: none -> 86.1 us  [shards(): lax.all_gather(jnp.stack(partial_pool).astype(jnp.bfloat16), 'dom')]
    unnamed x20 -> x25, local copies, waits for them, and re-layouts: 2.69 us -> 16.2 us
    reduce_sum x0 -> x1, other arithmetic: none -> 5.8 us  [shards(): jnp.sum(lax.all_gather(jnp.stack(partial_pool).astype(jnp.bfloat16), 'dom...]
  transfers between devices with their start and end apart: 10 -> 10, of which waited for: 7 -> 7; matrix products, arithmetic and copies ran while one was open for 6% -> 20% of each run, Pallas kernels for 0% -> 0%
where the time goes in v1:
time: 483 us; the launch traced here: 480 us
  waiting for transfers between devices  183 us (38%)
  loops' own time  109 us (23%)
  matrix products  61.4 us (13%)
  local copies, waits for them, and re-layouts  40.6 us (8%)
  starting transfers between devices  38 us (8%)
  other arithmetic  32.3 us (7%)
  between operations  15.1 us (3%)
    another operation x1, loops' own time, shards(): totals = lax.fori_loop(0, tile_used[s, 0], add_tile, totals)  108 us
    ppermute x7, waiting for transfers between devices, shifted(): return lax.ppermute(block, axis, route)  92.4 us
    all_gather x1, waiting for transfers between devices, shards(): lax.all_gather(jnp.stack(partial_pool).astype(jnp.bfloat16), 'dom')  86.1 us
    dot_general x24, matrix products, add_tile(): jnp.dot(tile_vals[s, j], source_of(s, j), preferred_element_type=jnp.floa...  41.3 us
    ppermute x7, starting transfers between devices, shifted(): return lax.ppermute(block, axis, route)  25.4 us
    another operation x24, other arithmetic  17.3 us
    unnamed x25, local copies, waits for them, and re-layouts  16.2 us
    dynamic_slice x24, local copies, waits for them, and re-layouts, source_of(): return fetched[owner_dev[s, j], s]  14.4 us
  transfers between devices with their start and end apart: 10, of which 7 were waited for; matrix products, arithmetic and copies ran while one was open for 20% of the time, Pallas kernels for 0%

profile of v1, /device:TPU:162, one launch (start us, length us, event | category | flops | bytes accessed | tf_op | source)
XLA Modules:
  0.0 479.8 jit_solution(8554582464251334824)
XLA Ops:
  7.2 2.8 fusion.220
  10.7 86.1 %all-gather.3.cloned.1.call-done = bf16[16384,512]{0,1:T(8,128)(2,1)} async-done(((bf16[512,512]{0,1:T(8,128)(2,1)}), bf16[16384,512]{0,1:T(8,128)(2,1)}) %all-gather.3.cloned.1.call-update) | async-done | bytes 16777232 | tf_op jit(solution)/shard_map/all_gather | solution.py:82
  96.9 12.1 %copy.168 = bf16[64,8,32,512]{3,2,1,0:T(8,128)(2,1)S(1)} copy(bf16[64,8,32,512]{3,1,2,0:T(8,128)(2,1)} %bitcast.369) | data formatting | bytes 33554432
  109.0 5.8 %bitcast_reduce_fusion = bf16[512,512]{0,1:T(8,128)(2,1)S(1)} fusion(bf16[64,8,32,512]{3,2,1,0:T(8,128)(2,1)S(1)} %copy.168), kind=kLoop, calls=%fused_computation.230 | loop fusion | flops 8126464 | bytes 17301504 | tf_op jit(solution)/shard_map/reduce_sum | solution.py:81
  114.8 2.7 convolution_bitcast_fusion.8
  121.2 6.7 %all-to-all-start = ((s32[32,1,1]{2,1,0:T(1,128)}), s32[32,1,1]{2,1,0:T(1,128)S(1)}, u32[]{:S(2)}, u32[]{:S(2)}) async-start(s32[32,1,1]{2,1,0:T(1,128)} %copy.126), calls=%async_computation | async-start | bytes 32768 | tf_op jit(solution)/shard_map/all_to_all | solution.py:58
  129.2 4.8 %all-to-all-done = s32[32,1,1]{2,1,0:T(1,128)S(1)} async-done(((s32[32,1,1]{2,1,0:T(1,128)}), s32[32,1,1]{2,1,0:T(1,128)S(1)}, u32[]{:S(2)}, u32[]{:S(2)}) %all-to-all-start) | async-done | bytes 160 | tf_op jit(solution)/shard_map/all_to_all | solution.py:58
  135.4 2.8 gather_fusion
  142.5 4.7 bitcast_select_fusion
  147.1 5.9 %all-to-all-start.1 = ((bf16[32,1,128,512]{3,2,1,0:T(8,128)(2,1)}), bf16[32,1,128,512]{3,2,1,0:T(8,128)(2,1)}, u32[]{:S(2)}, u32[]{:S(2)}) async-start(bf16[32,1,128,512]{3,2,1,0:T(8,128)(2,1)} %bitcast_select_fusion), calls=%async_computation.1 | async-start | bytes 8388608 | tf_op jit(solution)/shard_map/all_to_all | solution.py:60
  156.3 2.6 collective-permute-start.2
  158.8 13.0 %collective-permute-done.2 = bf16[512,512]{0,1:T(8,128)(2,1)S(1)} collective-permute-done((bf16[512,512]{0,1:T(8,128)(2,1)S(1)}, bf16[512,512]{0,1:T(8,128)(2,1)S(1)}, u32[]{:S(2)}, u32[]{:S(2)}) %collective-permute-start.2) | collective-permute-done | bytes 524320 | tf_op jit(solution)/shard_map/ppermute | solution.py:12
  174.4 13.2 %collective-permute-done.3 = bf16[512,512]{0,1:T(8,128)(2,1)S(1)} collective-permute-done((bf16[512,512]{0,1:T(8,128)(2,1)S(1)}, bf16[512,512]{0,1:T(8,128)(2,1)S(1)}, u32[]{:S(2)}, u32[]{:S(2)}) %collective-permute-start.3) | collective-permute-done | bytes 524320 | tf_op jit(solution)/shard_map/ppermute | solution.py:12
  190.2 52.4 %collective-permute-done.4 = bf16[512,512]{0,1:T(8,128)(2,1)S(1)} collective-permute-done((bf16[512,512]{0,1:T(8,128)(2,1)S(1)}, bf16[512,512]{0,1:T(8,128)(2,1)S(1)}, u32[]{:S(2)}, u32[]{:S(2)}) %collective-permute-start.4) | collective-permute-done | bytes 524320 | tf_op jit(solution)/shard_map/ppermute | solution.py:12
  242.7 10.0 %conditional.12 = (bf16[512,512]{1,0:T(8,128)(2,1)S(1)}) conditional(s32[]{:T(128)} %convert_element_type.160, (f32[512,512]{0,1:T(8,128)S(1)}) %tuple.103, (f32[1,3,512,512]{2,3,1,0:T(8,128)}, bf16[3,512,512]{2,1,0:T(8,128)(2,1)}, f32[512,512]{0,1:T(8,128)S(1)}, f32[512]{0:T(512)S(1)}) %tuple.144), branch_computations={%region_15.16_spmd, %region_16.17_spmd} | conditional | flops 810287104 | bytes 19925000 | solution.py:96
  242.7 3.6 copy.147
  246.6 3.0 fusion.161
  249.5 3.1 fusion.151
  254.9 11.4 %collective-permute-done.5 = bf16[512,512]{0,1:T(8,128)(2,1)} collective-permute-done((bf16[512,512]{0,1:T(8,128)(2,1)S(1)}, bf16[512,512]{0,1:T(8,128)(2,1)}, u32[]{:S(2)}, u32[]{:S(2)}) %collective-permute-start.5) | collective-permute-done | bytes 524320 | tf_op jit(solution)/shard_map/ppermute | solution.py:12
  268.2 12.0 %collective-permute-start.6 = (bf16[512,512]{0,1:T(8,128)(2,1)S(1)}, bf16[512,512]{0,1:T(8,128)(2,1)}, u32[]{:S(2)}, u32[]{:S(2)}) collective-permute-start(bf16[512,512]{0,1:T(8,128)(2,1)S(1)} %copy.153), channel_id=1, source_target_pairs={{0,1},{1,2},{2,3},{3,4},{4,5},{5,6},{6,7},{8,9},{9,10},{10,11},{11... | collective-permute-start | bytes 1572872 | tf_op jit(solution)/shard_map/ppermute | solution.py:12
  280.1 181.4 %while.11 = (s32[]{:T(128)}, f32[2,128,512]{2,1,0:T(8,128)S(1)}, s32[]{:T(128)}, s32[1,24]{1,0:T(1,128)S(1)}, bf16[1,24,128,128]{3,2,1,0:T(8,128)(2,1)}, /*index...) while((s32[]{:T(128)}, f32[2,128,512]{2,1,0:T(8,128)S(1)}, ...), condition=%wide.region_3.4_spmd, body=%wide.region_1.3_spmd.sunk | while | flops 16908316 | bytes 689436 | solution.py:72
  461.7 3.3 fusion.218
  464.9 4.3 multiply_add_fusion
  469.2 2.7 copy.154
  (143 shorter events, 98.5 us)
Async XLA Ops:
  7.2 107.6 %copy-start = (bf16[3,512,512]{2,1,0:T(8,128)(2,1)S(1)}, bf16[3,512,512]{2,1,0:T(8,128)(2,1)}, u32[]{:S(2)}) copy-start(bf16[3,512,512]{2,1,0:T(8,128)(2,1)} %param.34) | copy-start | bytes 4718596
  7.2 3.5 copy-start.11
  7.2 89.7 %all-gather.3.cloned.1.call-start = ((), (), s32[]{:S(2)}) async-start(), calls=%async_computation.2 | async-start | bytes 17301504 | tf_op jit(solution)/shard_map/all_gather | solution.py:82
  114.8 2.7 copy-start.3
  114.8 2.7 copy-start.10
  117.6 17.8 %copy-start.2 = (bf16[1,256,512]{2,1,0:T(8,128)(2,1)S(1)}, bf16[1,256,512]{2,1,0:T(8,128)(2,1)}, u32[]{:S(2)}) copy-start(bf16[1,256,512]{2,1,0:T(8,128)(2,1)} %param.28) | copy-start | bytes 786436
  117.8 20.4 %collective-permute-start = (bf16[512,512]{0,1:T(8,128)(2,1)S(1)}, bf16[512,512]{0,1:T(8,128)(2,1)}, u32[]{:S(2)}, u32[]{:S(2)}) collective-permute-start(bf16[512,512]{0,1:T(8,128)(2,1)S(1)} %copy.128), channel_id=1, source_target_pairs={{0,1},{1,2},{2,3},{3,4},{4,5},{5,6},{6,7},{8,9},{9,10},{10,11},{11... | collective-permute-start | bytes 1572872 | tf_op jit(solution)/shard_map/ppermute | solution.py:12
  121.2 12.8 %all-to-all-start = ((s32[32,1,1]{2,1,0:T(1,128)}), s32[32,1,1]{2,1,0:T(1,128)S(1)}, u32[]{:S(2)}, u32[]{:S(2)}) async-start(s32[32,1,1]{2,1,0:T(1,128)} %copy.126), calls=%async_computation | async-start | bytes 32768 | tf_op jit(solution)/shard_map/all_to_all | solution.py:58
  135.4 2.9 copy-start.4
  139.9 15.6 %collective-permute-start.1 = (bf16[512,512]{0,1:T(8,128)(2,1)S(1)}, bf16[512,512]{0,1:T(8,128)(2,1)S(1)}, u32[]{:S(2)}, u32[]{:S(2)}) collective-permute-start(bf16[512,512]{0,1:T(8,128)(2,1)S(1)} %copy.133), channel_id=1, source_target_pairs={{0,1},{1,2},{2,3},{3,4},{4,5},{5,6},{6,7},{8,9},{9,10},{10,11},{11... | collective-permute-start | bytes 1572872 | tf_op jit(solution)/shard_map/ppermute | solution.py:12
  147.1 133.0 %all-to-all-start.1 = ((bf16[32,1,128,512]{3,2,1,0:T(8,128)(2,1)}), bf16[32,1,128,512]{3,2,1,0:T(8,128)(2,1)}, u32[]{:S(2)}, u32[]{:S(2)}) async-start(bf16[32,1,128,512]{3,2,1,0:T(8,128)(2,1)} %bitcast_select_fusion), calls=%async_computation.1 | async-start | bytes 8388608 | tf_op jit(solution)/shard_map/all_to_all | solution.py:60
  156.3 15.6 %collective-permute-start.2 = (bf16[512,512]{0,1:T(8,128)(2,1)S(1)}, bf16[512,512]{0,1:T(8,128)(2,1)S(1)}, u32[]{:S(2)}, u32[]{:S(2)}) collective-permute-start(bf16[512,512]{0,1:T(8,128)(2,1)S(1)} %copy.137), channel_id=1, source_target_pairs={{0,1},{1,2},{2,3},{3,4},{4,5},{5,6},{6,7},{8,9},{9,10},{10,11},{11... | collective-permute-start | bytes 1572872 | tf_op jit(solution)/shard_map/ppermute | solution.py:12
  172.4 15.2 %collective-permute-start.3 = (bf16[512,512]{0,1:T(8,128)(2,1)S(1)}, bf16[512,512]{0,1:T(8,128)(2,1)S(1)}, u32[]{:S(2)}, u32[]{:S(2)}) collective-permute-start(bf16[512,512]{0,1:T(8,128)(2,1)S(1)} %copy.141), channel_id=1, source_target_pairs={{0,1},{1,2},{2,3},{3,4},{4,5},{5,6},{6,7},{8,9},{9,10},{10,11},{11... | collective-permute-start | bytes 1572872 | tf_op jit(solution)/shard_map/ppermute | solution.py:12
  188.2 54.3 %collective-permute-start.4 = (bf16[512,512]{0,1:T(8,128)(2,1)S(1)}, bf16[512,512]{0,1:T(8,128)(2,1)S(1)}, u32[]{:S(2)}, u32[]{:S(2)}) collective-permute-start(bf16[512,512]{0,1:T(8,128)(2,1)S(1)} %copy.145), channel_id=1, source_target_pairs={{0,1},{1,2},{2,3},{3,4},{4,5},{5,6},{6,7},{8,9},{9,10},{10,11},{11... | collective-permute-start | bytes 1572872 | tf_op jit(solution)/shard_map/ppermute | solution.py:12
  252.7 2.2 copy-start.12
  252.9 13.4 %collective-permute-start.5 = (bf16[512,512]{0,1:T(8,128)(2,1)S(1)}, bf16[512,512]{0,1:T(8,128)(2,1)}, u32[]{:S(2)}, u32[]{:S(2)}) collective-permute-start(bf16[512,512]{0,1:T(8,128)(2,1)S(1)} %copy.149), channel_id=1, source_target_pairs={{0,1},{1,2},{2,3},{3,4},{4,5},{5,6},{6,7},{8,9},{9,10},{10,11},{11... | collective-permute-start | bytes 1572872 | tf_op jit(solution)/shard_map/ppermute | solution.py:12
  267.5 12.7 %copy-start.8 = (s32[3]{0:T(128)S(1)}, s32[3]{0:T(128)}, u32[]{:S(2)}) copy-start(s32[3]{0:T(128)} %constant.92.clone.1) | copy-start | bytes 40
  268.2 193.5 %collective-permute-start.6 = (bf16[512,512]{0,1:T(8,128)(2,1)S(1)}, bf16[512,512]{0,1:T(8,128)(2,1)}, u32[]{:S(2)}, u32[]{:S(2)}) collective-permute-start(bf16[512,512]{0,1:T(8,128)(2,1)S(1)} %copy.153), channel_id=1, source_target_pairs={{0,1},{1,2},{2,3},{3,4},{4,5},{5,6},{6,7},{8,9},{9,10},{10,11},{11... | collective-permute-start | bytes 1572872 | tf_op jit(solution)/shard_map/ppermute | solution.py:12
  461.6 3.3 copy-start.9
  469.2 2.7 copy-start.5
  469.2 3.7 copy-start.1
Sparse Core Ops, SparseCore 0:
  11.0 85.7 all-gather.2
